TPU v7x, 512 devices: a whole 4x4x16 slice. The times are simulated.
512 devices in a mesh: gx: 8 (over x, core), gy: 8 (over z_hi, y), gz: 8 (over z_lo).
Axes of the slice: x: 4, y: 4, z: 16 (z_hi: 2, z_lo: 8; z = z_hi * 8 + z_lo), core: 2. Of those that a mesh axis runs over, the one named last changes fastest.
Arguments:
- magnet: float32 [3, 32, 256, 2048], P(None, 'gz', 'gx', 'gy'), may hold values from -1 to 1, as said below
- grains: int32 [32, 256, 2048], P('gz', 'gx', 'gy'), may hold values from 0 to 15
- stiffness_table: float32 [16], replicated, may hold values from 0.2 to 1
- saturation_table: float32 [16], replicated, may hold values from 0.6 to 1.4
- kernel_x: bfloat16 [8, 256], replicated, may hold values from -3 to 3
- kernel_y: bfloat16 [8, 2048], replicated, may hold values from -3 to 3
- kernel_z: bfloat16 [8, 32], replicated, may hold values from -3 to 3
- mixing: float32 [8, 3, 3], replicated, may hold values from -1.25 to 1.25
Outputs:
- magnet_next: float32 [3, 32, 256, 2048], P(None, 'gz', 'gx', 'gy')
- demag_field: float32 [16, 3, 128, 1024], P('gz', None, 'gx', 'gy')
Inputs may be any that keep to these rules, and one draw needn't show every extreme that they name: `magnet`: every cell's three components form a unit vector.
All inputs are finite; a program needn't handle non-finite values.
Results may differ from a plain program's by a relative error of at most 0.00085.
The roundings to bfloat16 on the way count: a program that leaves them out, or rounds other values in their place, can miss the bound.
Values may be sent and summed in bfloat16 or wider, within the bound.
No kernel may reach another device: no remote copies, remote signals or barrier semaphores. Data moves between devices by JAX's collectives and lax.ppermute only.
A program may use at most 128 MiB of HBM per device.

v0:
```python
import jax
import jax.numpy as jnp
from jax import lax
from jax.sharding import PartitionSpec as P

SUBSTEPS = 3
time_step = 0.02
damping = 0.3


def with_halo(x, sides, width):
    for axis, dim in sides:
        count, length = (lax.axis_size(axis), x.shape[dim])
        up = [(i, (i + 1) % count) for i in range(count - 1)]
        down = [(j, i) for i, j in up]
        last = lax.slice_in_dim(x, length - width, length, axis=dim)
        leading = lax.slice_in_dim(x, 0, width, axis=dim)
        before = lax.ppermute(last, axis, up)
        after = lax.ppermute(leading, axis, down)
        x = jnp.concatenate([before, x, after], axis=dim)
    return x


def toeplitz_rows(kernel, offset, extent):
    length = kernel.shape[1] // 2
    flipped = kernel[:, ::-1]
    row_ids = offset + jnp.arange(extent, dtype=jnp.int32)
    picked = jax.vmap(
        lambda row_index: lax.dynamic_slice_in_dim(flipped, length - 1 - row_index, length, 1)
    )(row_ids)
    return jnp.transpose(picked, (1, 0, 2))


def interior(values):
    return values[..., 1:-1, 1:-1, 1:-1]


def shifted(values, along, begin_at):
    slicer = [slice(1, -1), slice(1, -1), slice(1, -1)]
    slicer[along] = slice(begin_at, begin_at + values.shape[along - 3] - 2)
    leading = [slice(None)] * (values.ndim - 3)
    return values[tuple(leading + slicer)]


def cross_product(first_vec, second_vec):
    return jnp.stack(
        [
            first_vec[1] * second_vec[2] - first_vec[2] * second_vec[1],
            first_vec[2] * second_vec[0] - first_vec[0] * second_vec[2],
            first_vec[0] * second_vec[1] - first_vec[1] * second_vec[0],
        ]
    )


def exchange_update(magnet_rim, stiff_rim, saturation, demag_fine):
    centre = interior(magnet_rim)
    stiff_centre = interior(stiff_rim)
    coupled = jnp.zeros_like(centre)
    for along in range(3):
        for begin_at in (0, 2):
            stiff_near = shifted(stiff_rim, along, begin_at)
            denominator = stiff_centre + stiff_near
            weight = (
                2.0 * stiff_centre * stiff_near / jnp.where(denominator > 0.0, denominator, 1.0)
            )
            coupled = coupled + weight[None] * (shifted(magnet_rim, along, begin_at) - centre)
    inside = saturation > 0.0
    safe_sat = jnp.where(inside, saturation, 1.0)
    field_total = 2.0 * coupled / safe_sat[None] + demag_fine
    torque = cross_product(centre, field_total)
    raw_next = centre - time_step * (torque + damping * cross_product(centre, torque))
    length_sq = jnp.sqrt(jnp.sum(raw_next * raw_next, axis=0))
    safe_len = jnp.where(inside, length_sq, 1.0)
    return jnp.where(inside[None], raw_next / safe_len[None], 0.0)


def coarsen(magnet, saturation):
    weighted = saturation[None] * magnet
    comps, depth, width, height = weighted.shape
    shaped = weighted.reshape(comps, depth // 2, 2, width // 2, 2, height // 2, 2)
    return jnp.mean(shaped, axis=(2, 4, 6)).astype(jnp.bfloat16)


def prolong(demag):
    moved = jnp.transpose(demag, (1, 0, 2, 3))
    return jnp.repeat(jnp.repeat(jnp.repeat(moved, 2, axis=1), 2, axis=2), 2, axis=3)


def material_field(grains, lookup):
    labels = jnp.arange(lookup.shape[0], dtype=jnp.int32)
    matches = grains[None] == labels[:, None, None, None]
    return jnp.sum(jnp.where(matches, lookup[:, None, None, None], 0.0), axis=0)


def local(magnet, grains, stiffness_table, saturation_table, kernel_x, kernel_y, kernel_z, mixing):
    stiffness = material_field(grains, stiffness_table)
    saturation = material_field(grains, saturation_table)
    coarse = coarsen(magnet, saturation)
    rows_z = coarse.shape[1]
    rows_x = coarse.shape[2]
    rows_y = coarse.shape[3]
    block_x = toeplitz_rows(kernel_x, lax.axis_index("gx") * rows_x, rows_x)
    columns = block_x
    along_x = jnp.einsum(
        "rab,jzby->rjzay",
        columns,
        lax.all_gather(coarse, "gx", axis=2, tiled=True),
        preferred_element_type=jnp.float32,
    ).astype(jnp.bfloat16)
    block_y = toeplitz_rows(kernel_y, lax.axis_index("gy") * rows_y, rows_y)
    columns = block_y
    along_y = jnp.einsum(
        "rby,rjzxy->rjzxb",
        columns,
        lax.all_gather(along_x, "gy", axis=4, tiled=True),
        preferred_element_type=jnp.float32,
    ).astype(jnp.bfloat16)
    whole_z = toeplitz_rows(kernel_z, 0, kernel_z.shape[1] // 2).astype(jnp.float32)
    offset = lax.axis_index("gz") * rows_z
    own_rows = lax.dynamic_slice_in_dim(whole_z, offset, rows_z, 1)
    weights = jnp.einsum("rij,raz->airjz", mixing, own_rows, precision=lax.Precision.HIGHEST)
    columns = weights
    demag = jnp.einsum(
        "airjz,rjzxy->aixy",
        columns,
        lax.all_gather(along_y, "gz", axis=2, tiled=True).astype(jnp.float32),
        precision=lax.Precision.HIGHEST,
    )
    demag_fine = prolong(demag)
    stiff_rim = with_halo(
        stiffness[None].astype(jnp.bfloat16), (("gx", 2), ("gy", 3), ("gz", 1)), 1
    ).astype(jnp.float32)[0]
    state = magnet
    for substep in range(SUBSTEPS):
        magnet_rim = with_halo(state, (("gx", 2), ("gy", 3), ("gz", 1)), 1)
        state = exchange_update(magnet_rim, stiff_rim, saturation, demag_fine)
    return (state, demag)


def solution(mesh):
    in_specs = (P(None, "gz", "gx", "gy"), P("gz", "gx", "gy"), P(), P(), P(), P(), P(), P())
    out_specs = (P(None, "gz", "gx", "gy"), P("gz", None, "gx", "gy"))
    return jax.shard_map(local, mesh=mesh, in_specs=in_specs, out_specs=out_specs, check_vma=False)
```

profile of v0, /device:TPU:320, one launch (start us, length us, event | category | flops | bytes accessed | tf_op | source)
XLA Modules:
  0.0 573.6 jit_solution(10090580710956281949)
XLA Ops:
  9.6 26.6 %reshape.132 = f32[3,2,2,16,2,128,2]{6,5,4,3,2,1,0:T(8,128)} reshape(f32[3,4,32,256]{3,2,1,0:T(8,128)S(1)} %broadcast_multiply_fusion) | data formatting | bytes 786432 | tf_op jit(solution)/shard_map/reshape | solution.py:80
  36.2 9.5 %reduce_sum.56 = f32[3,2,16,128]{3,2,1,0:T(8,128)S(1)} reduce(f32[3,2,2,16,2,128,2]{6,5,4,3,2,1,0:T(8,128)} %reshape.132, f32[]{:T(128)} %constant.19.clone.1), dimensions={2,4,6}, to_apply=%region_2.3 | reduce | flops 86016 | bytes 442372 | tf_op jit(solution)/shard_map/reduce_sum | solution.py:81
  45.6 13.2 %all_gather.9 = bf16[3,2,128,128]{3,2,1,0:T(8,128)(2,1)S(1)} all-gather(bf16[3,2,16,128]{3,2,1,0:T(8,128)(2,1)S(1)} %multiply_convert_fusion), channel_id=1, replica_groups=mesh['gx'=8,'gy'=8,'gz'=8] {'gx'}, dimensions={2}, use_global_device_ids=true | all-gather | bytes 221184 | tf_op jit(solution)/shard_map/all_gather | solution.py:107
  59.0 21.6 %while.4 = (s32[]{:T(128)}, bf16[8,256]{1,0:T(8,128)(2,1)S(1)}, s32[16,2]{0,1:T(2,128)S(1)}, bf16[16,8,128]{2,1,0:T(8,128)(2,1)S(1)}, s32[]{:T(128)}) while((s32[]{:T(128)}, bf16[8,256]{1,0:T(8,128)(2,1)S(1)}, s32[16,2]{0,1:T(2,128)S(1)}, bf16[16,8,128]{2,1,0:T(8,128)(2,1)S(1)}, s32[]{:T(128)}) %tuple.89), condition=%wide.while_cond.1, body=%wide.while_body.1.sunk | while | flops 2 | bytes 4201 | solution.py:29
  92.1 252.3 %while.5 = (s32[]{:T(128)}, bf16[8,2048]{1,0:T(8,128)(2,1)S(1)}, s32[128,2]{0,1:T(2,128)S(1)}, bf16[128,8,1024]{2,1,0:T(8,128)(2,1)}, s32[]{:T(128)}) while((s32[]{:T(128)}, bf16[8,2048]{1,0:T(8,128)(2,1)S(1)}, s32[128,2]{0,1:T(2,128)S(1)}, bf16[128,8,1024]{2,1,0:T(8,128)(2,1)}, s32[]{:T(128)}) %tuple.86), condition=%wide.while_cond.2, body=%wide.while_body.2.sunk | while | flops 2 | bytes 33381 | solution.py:29
  344.5 21.9 %while.3 = (s32[]{:T(128)}, bf16[8,32]{1,0:T(8,128)(2,1)S(1)}, s32[16,2]{0,1:T(2,128)S(1)}, bf16[16,8,16]{2,1,0:T(8,128)(2,1)S(1)}, s32[]{:T(128)}) while((s32[]{:T(128)}, bf16[8,32]{1,0:T(8,128)(2,1)S(1)}, s32[16,2]{0,1:T(2,128)S(1)}, bf16[16,8,16]{2,1,0:T(8,128)(2,1)S(1)}, s32[]{:T(128)}) %tuple.92), condition=%wide.while_cond, body=%wide.while_body.sunk | while | flops 2 | bytes 4201 | solution.py:29
  366.4 4.2 fusion.6
  376.9 14.6 %collective-permute-done.2 = bf16[1,4,34,1]{3,1,2,0:T(4,128)(2,1)S(1)} collective-permute-done((bf16[1,4,34,1]{3,1,2,0:T(4,128)(2,1)S(1)}, bf16[1,4,34,1]{3,1,2,0:T(4,128)(2,1)S(1)}, u32[]{:S(2)}, u32[]{:S(2)}) %collective-permute-start.2) | collective-permute-done | bytes 304 | tf_op jit(solution)/shard_map/ppermute | solution.py:18
  394.1 3.9 collective-permute-start.8
  400.1 3.9 collective-permute-start.4
  404.1 7.6 %collective-permute-done.9 = f32[3,4,34,1]{3,1,2,0:T(4,128)S(1)} collective-permute-done((f32[3,4,34,1]{3,1,2,0:T(4,128)S(1)}, f32[3,4,34,1]{3,1,2,0:T(4,128)S(1)}, u32[]{:S(2)}, u32[]{:S(2)}) %collective-permute-start.9) | collective-permute-done | bytes 1664 | tf_op jit(solution)/shard_map/ppermute | solution.py:19
  411.7 15.3 %collective-permute-done.8 = f32[3,4,34,1]{3,1,2,0:T(4,128)S(1)} collective-permute-done((f32[3,4,34,1]{3,1,2,0:T(4,128)S(1)}, f32[3,4,34,1]{3,1,2,0:T(4,128)S(1)}, u32[]{:S(2)}, u32[]{:S(2)}) %collective-permute-start.8) | collective-permute-done | bytes 1664 | tf_op jit(solution)/shard_map/ppermute | solution.py:18
  428.4 12.6 %collective-permute-start.11 = (f32[3,1,34,258]{3,2,1,0:T(8,128)}, f32[3,1,34,258]{3,2,1,0:T(8,128)}, u32[]{:S(2)}, u32[]{:S(2)}) collective-permute-start(f32[3,1,34,258]{3,2,1,0:T(8,128)} %get-tuple-element.96), channel_id=1, source_target_pairs={{1,0},{2,1},{3,2},{4,3},{5,4},{6,5},{7,6},{9,8},{10,9},{11,10},{12... | collective-permute-start | bytes 315800 | tf_op jit(solution)/shard_map/ppermute | solution.py:19
  457.9 4.2 collective-permute-done.13
  464.6 3.6 collective-permute-start.14
  470.8 13.5 %collective-permute-done.14 = f32[3,4,34,1]{3,1,2,0:T(4,128)S(1)} collective-permute-done((f32[3,4,34,1]{3,1,2,0:T(4,128)S(1)}, f32[3,4,34,1]{3,1,2,0:T(4,128)S(1)}, u32[]{:S(2)}, u32[]{:S(2)}) %collective-permute-start.14) | collective-permute-done | bytes 1664 | tf_op jit(solution)/shard_map/ppermute | solution.py:18
  484.9 16.8 %collective-permute-start.17 = (f32[3,1,34,258]{3,2,1,0:T(8,128)S(1)}, f32[3,1,34,258]{3,2,1,0:T(8,128)S(1)}, u32[]{:S(2)}, u32[]{:S(2)}) collective-permute-start(f32[3,1,34,258]{3,2,1,0:T(8,128)S(1)} %get-tuple-element.94), channel_id=1, source_target_pairs={{1,0},{2,1},{3,2},{4,3},{5,4},{6,5},{7,6},{9,8},{10,9},{11,10},{12... | collective-permute-start | bytes 315800 | tf_op jit(solution)/shard_map/ppermute | solution.py:19
  506.0 4.1 collective-permute-done.16
  514.2 4.1 collective-permute-done.19
  520.4 3.9 collective-permute-start.20
  525.0 4.0 collective-permute-done.21
  529.0 15.4 %collective-permute-done.20 = f32[3,4,34,1]{3,1,2,0:T(4,128)S(1)} collective-permute-done((f32[3,4,34,1]{3,1,2,0:T(4,128)S(1)}, f32[3,4,34,1]{3,1,2,0:T(4,128)S(1)}, u32[]{:S(2)}, u32[]{:S(2)}) %collective-permute-start.20) | collective-permute-done | bytes 1664 | tf_op jit(solution)/shard_map/ppermute | solution.py:18
  545.0 11.7 %collective-permute-start.23 = (f32[3,1,34,258]{3,2,1,0:T(8,128)S(1)}, f32[3,1,34,258]{3,2,1,0:T(8,128)S(1)}, u32[]{:S(2)}, u32[]{:S(2)}) collective-permute-start(f32[3,1,34,258]{3,2,1,0:T(8,128)S(1)} %get-tuple-element.92), channel_id=1, source_target_pairs={{1,0},{2,1},{3,2},{4,3},{5,4},{6,5},{7,6},{9,8},{10,9},{11,10},{12... | collective-permute-start | bytes 315800 | tf_op jit(solution)/shard_map/ppermute | solution.py:19
  560.8 4.1 collective-permute-done.22
  (637 shorter events, 361.7 us)
Async XLA Ops:
  7.2 359.3 %all-gather.3.cloned.1.call-start = ((), (), s32[]{:S(2)}) async-start(), calls=%async_computation | async-start | bytes 1769472 | tf_op jit(solution)/shard_map/all_gather | solution.py:115
  81.5 364.0 %all-gather.5.cloned.1.call-start = ((), (), s32[]{:S(2)}) async-start(), calls=%async_computation.1 | async-start | bytes 1769472 | tf_op jit(solution)/shard_map/all_gather | solution.py:126
  81.6 310.4 %collective-permute-start.7 = (f32[3,4,1,256]{3,1,2,0:T(4,128)S(1)}, f32[3,4,1,256]{3,1,2,0:T(4,128)S(1)}, u32[]{:S(2)}, u32[]{:S(2)}) collective-permute-start(f32[3,4,1,256]{3,1,2,0:T(4,128)S(1)} %copy.552), channel_id=1, source_target_pairs={{64,0},{128,64},{192,128},{256,192},{320,256},{384,320},{448,384},... | collective-permute-start | bytes 36872 | tf_op jit(solution)/shard_map/ppermute | solution.py:19
  82.9 308.8 %collective-permute-start.6 = (f32[3,4,1,256]{3,1,2,0:T(4,128)S(1)}, f32[3,4,1,256]{3,1,2,0:T(4,128)S(1)}, u32[]{:S(2)}, u32[]{:S(2)}) collective-permute-start(f32[3,4,1,256]{3,1,2,0:T(4,128)S(1)} %copy.553), channel_id=1, source_target_pairs={{0,64},{64,128},{128,192},{192,256},{256,320},{320,384},{384,448},... | collective-permute-start | bytes 36872 | tf_op jit(solution)/shard_map/ppermute | solution.py:18
  86.0 284.7 %collective-permute-start = (bf16[1,4,1,256]{3,2,1,0:T(2,128)(2,1)S(1)}, bf16[1,4,1,256]{3,2,1,0:T(2,128)(2,1)S(1)}, u32[]{:S(2)}, u32[]{:S(2)}) collective-permute-start(bf16[1,4,1,256]{3,2,1,0:T(2,128)(2,1)S(1)} %get-tuple-element.126), channel_id=1, source_target_pairs={{0,64},{64,128},{128,192},{192,256},{256,320},{320,384},{384,448},... | collective-permute-start | bytes 6152 | tf_op jit(solution)/shard_map/ppermute | solution.py:18
  89.5 281.3 %collective-permute-start.1 = (bf16[1,4,1,256]{3,2,1,0:T(2,128)(2,1)S(1)}, bf16[1,4,1,256]{3,2,1,0:T(2,128)(2,1)S(1)}, u32[]{:S(2)}, u32[]{:S(2)}) collective-permute-start(bf16[1,4,1,256]{3,2,1,0:T(2,128)(2,1)S(1)} %get-tuple-element.125), channel_id=1, source_target_pairs={{64,0},{128,64},{192,128},{256,192},{320,256},{384,320},{448,384},... | collective-permute-start | bytes 6152 | tf_op jit(solution)/shard_map/ppermute | solution.py:19
  370.9 6.0 %collective-permute-start.3 = (bf16[1,4,34,1]{3,1,2,0:T(4,128)(2,1)S(1)}, bf16[1,4,34,1]{3,1,2,0:T(4,128)(2,1)S(1)}, u32[]{:S(2)}, u32[]{:S(2)}) collective-permute-start(bf16[1,4,34,1]{3,1,2,0:T(4,128)(2,1)S(1)} %get-tuple-element.124), channel_id=1, source_target_pairs={{8,0},{16,8},{24,16},{32,24},{40,32},{48,40},{56,48},{9,1},{17,9},... | collective-permute-start | bytes 824 | tf_op jit(solution)/shard_map/ppermute | solution.py:19
  374.0 17.5 %collective-permute-start.2 = (bf16[1,4,34,1]{3,1,2,0:T(4,128)(2,1)S(1)}, bf16[1,4,34,1]{3,1,2,0:T(4,128)(2,1)S(1)}, u32[]{:S(2)}, u32[]{:S(2)}) collective-permute-start(bf16[1,4,34,1]{3,1,2,0:T(4,128)(2,1)S(1)} %get-tuple-element.123), channel_id=1, source_target_pairs={{0,8},{8,16},{16,24},{24,32},{32,40},{40,48},{48,56},{1,9},{9,17},... | collective-permute-start | bytes 824 | tf_op jit(solution)/shard_map/ppermute | solution.py:18
  392.2 19.5 %collective-permute-start.9 = (f32[3,4,34,1]{3,1,2,0:T(4,128)S(1)}, f32[3,4,34,1]{3,1,2,0:T(4,128)S(1)}, u32[]{:S(2)}, u32[]{:S(2)}) collective-permute-start(f32[3,4,34,1]{3,1,2,0:T(4,128)S(1)} %get-tuple-element.108), channel_id=1, source_target_pairs={{8,0},{16,8},{24,16},{32,24},{40,32},{48,40},{56,48},{9,1},{17,9},... | collective-permute-start | bytes 4904 | tf_op jit(solution)/shard_map/ppermute | solution.py:19
  394.1 32.9 %collective-permute-start.8 = (f32[3,4,34,1]{3,1,2,0:T(4,128)S(1)}, f32[3,4,34,1]{3,1,2,0:T(4,128)S(1)}, u32[]{:S(2)}, u32[]{:S(2)}) collective-permute-start(f32[3,4,34,1]{3,1,2,0:T(4,128)S(1)} %get-tuple-element.107), channel_id=1, source_target_pairs={{0,8},{8,16},{16,24},{24,32},{32,40},{40,48},{48,56},{1,9},{9,17},... | collective-permute-start | bytes 4904 | tf_op jit(solution)/shard_map/ppermute | solution.py:18
  398.2 46.2 %collective-permute-start.5 = (bf16[1,1,34,258]{3,2,1,0:T(8,128)(2,1)S(1)}, bf16[1,1,34,258]{3,2,1,0:T(8,128)(2,1)S(1)}, u32[]{:S(2)}, u32[]{:S(2)}) collective-permute-start(bf16[1,1,34,258]{3,2,1,0:T(8,128)(2,1)S(1)} %copy.554), channel_id=1, source_target_pairs={{1,0},{2,1},{3,2},{4,3},{5,4},{6,5},{7,6},{9,8},{10,9},{11,10},{12... | collective-permute-start | bytes 52640 | tf_op jit(solution)/shard_map/ppermute | solution.py:19
  400.1 44.3 %collective-permute-start.4 = (bf16[1,1,34,258]{3,2,1,0:T(8,128)(2,1)S(1)}, bf16[1,1,34,258]{3,2,1,0:T(8,128)(2,1)S(1)}, u32[]{:S(2)}, u32[]{:S(2)}) collective-permute-start(bf16[1,1,34,258]{3,2,1,0:T(8,128)(2,1)S(1)} %copy.555), channel_id=1, source_target_pairs={{0,1},{1,2},{2,3},{3,4},{4,5},{5,6},{6,7},{8,9},{9,10},{10,11},{11... | collective-permute-start | bytes 52640 | tf_op jit(solution)/shard_map/ppermute | solution.py:18
  428.4 24.0 %collective-permute-start.11 = (f32[3,1,34,258]{3,2,1,0:T(8,128)}, f32[3,1,34,258]{3,2,1,0:T(8,128)}, u32[]{:S(2)}, u32[]{:S(2)}) collective-permute-start(f32[3,1,34,258]{3,2,1,0:T(8,128)} %get-tuple-element.96), channel_id=1, source_target_pairs={{1,0},{2,1},{3,2},{4,3},{5,4},{6,5},{7,6},{9,8},{10,9},{11,10},{12... | collective-permute-start | bytes 315800 | tf_op jit(solution)/shard_map/ppermute | solution.py:19
  441.0 11.4 %collective-permute-start.10 = (f32[3,1,34,258]{3,2,1,0:T(8,128)}, f32[3,1,34,258]{3,2,1,0:T(8,128)}, u32[]{:S(2)}, u32[]{:S(2)}) collective-permute-start(f32[3,1,34,258]{3,2,1,0:T(8,128)} %get-tuple-element.95), channel_id=1, source_target_pairs={{0,1},{1,2},{2,3},{3,4},{4,5},{5,6},{6,7},{8,9},{9,10},{10,11},{11... | collective-permute-start | bytes 315800 | tf_op jit(solution)/shard_map/ppermute | solution.py:18
  456.1 6.0 %collective-permute-start.13 = (f32[3,4,1,256]{3,1,2,0:T(4,128)S(1)}, f32[3,4,1,256]{3,1,2,0:T(4,128)S(1)}, u32[]{:S(2)}, u32[]{:S(2)}) collective-permute-start(f32[3,4,1,256]{3,1,2,0:T(4,128)S(1)} %copy.455), channel_id=1, source_target_pairs={{64,0},{128,64},{192,128},{256,192},{320,256},{384,320},{448,384},... | collective-permute-start | bytes 36872 | tf_op jit(solution)/shard_map/ppermute | solution.py:19
  462.3 8.5 %collective-permute-start.15 = (f32[3,4,34,1]{3,1,2,0:T(4,128)S(1)}, f32[3,4,34,1]{3,1,2,0:T(4,128)S(1)}, u32[]{:S(2)}, u32[]{:S(2)}) collective-permute-start(f32[3,4,34,1]{3,1,2,0:T(4,128)S(1)} %get-tuple-element.104), channel_id=1, source_target_pairs={{8,0},{16,8},{24,16},{32,24},{40,32},{48,40},{56,48},{9,1},{17,9},... | collective-permute-start | bytes 4904 | tf_op jit(solution)/shard_map/ppermute | solution.py:19
  464.6 19.7 %collective-permute-start.14 = (f32[3,4,34,1]{3,1,2,0:T(4,128)S(1)}, f32[3,4,34,1]{3,1,2,0:T(4,128)S(1)}, u32[]{:S(2)}, u32[]{:S(2)}) collective-permute-start(f32[3,4,34,1]{3,1,2,0:T(4,128)S(1)} %get-tuple-element.103), channel_id=1, source_target_pairs={{0,8},{8,16},{16,24},{24,32},{32,40},{40,48},{48,56},{1,9},{9,17},... | collective-permute-start | bytes 4904 | tf_op jit(solution)/shard_map/ppermute | solution.py:18
  484.9 21.1 %collective-permute-start.17 = (f32[3,1,34,258]{3,2,1,0:T(8,128)S(1)}, f32[3,1,34,258]{3,2,1,0:T(8,128)S(1)}, u32[]{:S(2)}, u32[]{:S(2)}) collective-permute-start(f32[3,1,34,258]{3,2,1,0:T(8,128)S(1)} %get-tuple-element.94), channel_id=1, source_target_pairs={{1,0},{2,1},{3,2},{4,3},{5,4},{6,5},{7,6},{9,8},{10,9},{11,10},{12... | collective-permute-start | bytes 315800 | tf_op jit(solution)/shard_map/ppermute | solution.py:19
  501.7 8.5 %collective-permute-start.16 = (f32[3,1,34,258]{3,2,1,0:T(8,128)S(1)}, f32[3,1,34,258]{3,2,1,0:T(8,128)S(1)}, u32[]{:S(2)}, u32[]{:S(2)}) collective-permute-start(f32[3,1,34,258]{3,2,1,0:T(8,128)S(1)} %get-tuple-element.93), channel_id=1, source_target_pairs={{0,1},{1,2},{2,3},{3,4},{4,5},{5,6},{6,7},{8,9},{9,10},{10,11},{11... | collective-permute-start | bytes 315800 | tf_op jit(solution)/shard_map/ppermute | solution.py:18
  512.6 5.7 %collective-permute-start.19 = (f32[3,4,1,256]{3,1,2,0:T(4,128)S(1)}, f32[3,4,1,256]{3,1,2,0:T(4,128)S(1)}, u32[]{:S(2)}, u32[]{:S(2)}) collective-permute-start(f32[3,4,1,256]{3,1,2,0:T(4,128)S(1)} %copy.469), channel_id=1, source_target_pairs={{64,0},{128,64},{192,128},{256,192},{320,256},{384,320},{448,384},... | collective-permute-start | bytes 36872 | tf_op jit(solution)/shard_map/ppermute | solution.py:19
  518.5 10.5 %collective-permute-start.21 = (f32[3,4,34,1]{3,1,2,0:T(4,128)S(1)}, f32[3,4,34,1]{3,1,2,0:T(4,128)S(1)}, u32[]{:S(2)}, u32[]{:S(2)}) collective-permute-start(f32[3,4,34,1]{3,1,2,0:T(4,128)S(1)} %get-tuple-element.100), channel_id=1, source_target_pairs={{8,0},{16,8},{24,16},{32,24},{40,32},{48,40},{56,48},{9,1},{17,9},... | collective-permute-start | bytes 4904 | tf_op jit(solution)/shard_map/ppermute | solution.py:19
  520.4 24.0 %collective-permute-start.20 = (f32[3,4,34,1]{3,1,2,0:T(4,128)S(1)}, f32[3,4,34,1]{3,1,2,0:T(4,128)S(1)}, u32[]{:S(2)}, u32[]{:S(2)}) collective-permute-start(f32[3,4,34,1]{3,1,2,0:T(4,128)S(1)} %get-tuple-element.99), channel_id=1, source_target_pairs={{0,8},{8,16},{16,24},{24,32},{32,40},{40,48},{48,56},{1,9},{9,17},... | collective-permute-start | bytes 4904 | tf_op jit(solution)/shard_map/ppermute | solution.py:18
  545.0 15.8 %collective-permute-start.23 = (f32[3,1,34,258]{3,2,1,0:T(8,128)S(1)}, f32[3,1,34,258]{3,2,1,0:T(8,128)S(1)}, u32[]{:S(2)}, u32[]{:S(2)}) collective-permute-start(f32[3,1,34,258]{3,2,1,0:T(8,128)S(1)} %get-tuple-element.92), channel_id=1, source_target_pairs={{1,0},{2,1},{3,2},{4,3},{5,4},{6,5},{7,6},{9,8},{10,9},{11,10},{12... | collective-permute-start | bytes 315800 | tf_op jit(solution)/shard_map/ppermute | solution.py:19
  556.7 8.3 %collective-permute-start.22 = (f32[3,1,34,258]{3,2,1,0:T(8,128)S(1)}, f32[3,1,34,258]{3,2,1,0:T(8,128)S(1)}, u32[]{:S(2)}, u32[]{:S(2)}) collective-permute-start(f32[3,1,34,258]{3,2,1,0:T(8,128)S(1)} %get-tuple-element.91), channel_id=1, source_target_pairs={{0,1},{1,2},{2,3},{3,4},{4,5},{5,6},{6,7},{8,9},{9,10},{10,11},{11... | collective-permute-start | bytes 315800 | tf_op jit(solution)/shard_map/ppermute | solution.py:18
  (13 other events, 562.1 us)
Sparse Core Ops, SparseCore 0:
  81.6 92.3 all-gather.2
  370.8 70.4 all-gather.4
where the time goes:
time: 576 us; the launch traced here: 574 us
  local copies, waits for them, and re-layouts  331 us (57%)
  waiting for transfers between devices  93.2 us (16%)
  starting transfers between devices  90.5 us (16%)
  other arithmetic  22.3 us (4%)
  between operations  14.9 us (3%)
  blocking collectives  13.2 us (2%)
  matrix products  7.96 us (1%)
    gather x480, local copies, waits for them, and re-layouts  296 us
    ppermute x12, waiting for transfers between devices, with_halo(): before = lax.ppermute(last, axis, up)  67 us
    ppermute x12, starting transfers between devices, with_halo(): after = lax.ppermute(leading, axis, down)  57.4 us
    ppermute x12, starting transfers between devices, with_halo(): before = lax.ppermute(last, axis, up)  33 us
    reshape x1, local copies, waits for them, and re-layouts, coarsen(): weighted.reshape(comps, depth // 2, 2, width // 2, 2, height // 2, 2)  26.6 us
    ppermute x12, waiting for transfers between devices, with_halo(): after = lax.ppermute(leading, axis, down)  26.1 us
    all_gather x1, blocking collectives, local(): lax.all_gather(coarse, 'gx', axis=2, tiled=True)  13.2 us
  transfers between devices with their start and end apart: 26, of which 14 were waited for; matrix products, arithmetic and copies ran while one was open for 51% of the time, Pallas kernels for 0%

commit v1 on v0

--- a/solution.py
+++ b/solution.py
@@ -104,7 +104,9 @@
     along_x = jnp.einsum(
         "rab,jzby->rjzay",
         columns,
-        lax.all_gather(coarse, "gx", axis=2, tiled=True),
+        jnp.concatenate(
+            lax.all_to_all(jnp.stack([coarse] * lax.axis_size("gx")), "gx", 0, 0), axis=2
+        ),
         preferred_element_type=jnp.float32,
     ).astype(jnp.bfloat16)
     block_y = toeplitz_rows(kernel_y, lax.axis_index("gy") * rows_y, rows_y)

time: 576 us -> 641 us (1.11)
  the two profiles are of different devices: /device:TPU:320 before, /device:TPU:322 now
where the time goes in v1:
time: 641 us; the launch traced here: 638 us
  local copies, waits for them, and re-layouts  330 us (51%)
  waiting for transfers between devices  157 us (24%)
  starting transfers between devices  106 us (17%)
  other arithmetic  22.3 us (3%)
  between operations  14.9 us (2%)
  matrix products  7.97 us (1%)
    gather x480, local copies, waits for them, and re-layouts  294 us
    all_gather x1, waiting for transfers between devices, local(): lax.all_gather(along_x, 'gy', axis=4, tiled=True)  70 us
    ppermute x12, starting transfers between devices, with_halo(): after = lax.ppermute(leading, axis, down)  68.7 us
    ppermute x12, waiting for transfers between devices, with_halo(): before = lax.ppermute(last, axis, up)  67.2 us
    ppermute x12, starting transfers between devices, with_halo(): before = lax.ppermute(last, axis, up)  32.1 us
    reshape x1, local copies, waits for them, and re-layouts, coarsen(): weighted.reshape(comps, depth // 2, 2, width // 2, 2, height // 2, 2)  26.5 us
    ppermute x12, waiting for transfers between devices, with_halo(): after = lax.ppermute(leading, axis, down)  19.6 us
  transfers between devices with their start and end apart: 27, of which 14 were waited for; matrix products, arithmetic and copies ran while one was open for 49% of the time, Pallas kernels for 0%

profile of v1, /device:TPU:322, one launch (start us, length us, event | category | flops | bytes accessed | tf_op | source)
XLA Modules:
  0.0 638.2 jit_solution(877827879802203518)
XLA Ops:
  9.5 26.5 %reshape.140 = f32[3,2,2,16,2,128,2]{6,5,4,3,2,1,0:T(8,128)} reshape(f32[3,4,32,256]{3,2,1,0:T(8,128)S(1)} %broadcast_multiply_fusion) | data formatting | bytes 786432 | tf_op jit(solution)/shard_map/reshape | solution.py:80
  36.1 9.4 %reduce_sum.56 = f32[3,2,16,128]{3,2,1,0:T(8,128)S(1)} reduce(f32[3,2,2,16,2,128,2]{6,5,4,3,2,1,0:T(8,128)} %reshape.140, f32[]{:T(128)} %constant.19.clone.1), dimensions={2,4,6}, to_apply=%region_2.3 | reduce | flops 86016 | bytes 442372 | tf_op jit(solution)/shard_map/reduce_sum | solution.py:81
  46.3 4.8 all-to-all-start
  62.4 249.4 %while.5 = (s32[]{:T(128)}, bf16[8,2048]{1,0:T(8,128)(2,1)S(1)}, s32[128,2]{0,1:T(2,128)S(1)}, bf16[128,8,1024]{2,1,0:T(8,128)(2,1)}, s32[]{:T(128)}) while((s32[]{:T(128)}, bf16[8,2048]{1,0:T(8,128)(2,1)S(1)}, s32[128,2]{0,1:T(2,128)S(1)}, bf16[128,8,1024]{2,1,0:T(8,128)(2,1)}, s32[]{:T(128)}) %tuple.86), condition=%wide.while_cond.2, body=%wide.while_body.2.sunk | while | flops 2 | bytes 33381 | solution.py:29
  312.0 21.7 %while.4 = (s32[]{:T(128)}, bf16[8,256]{1,0:T(8,128)(2,1)S(1)}, s32[16,2]{0,1:T(2,128)S(1)}, bf16[16,8,128]{2,1,0:T(8,128)(2,1)S(1)}, s32[]{:T(128)}) while((s32[]{:T(128)}, bf16[8,256]{1,0:T(8,128)(2,1)S(1)}, s32[16,2]{0,1:T(2,128)S(1)}, bf16[16,8,128]{2,1,0:T(8,128)(2,1)S(1)}, s32[]{:T(128)}) %tuple.89), condition=%wide.while_cond.1, body=%wide.while_body.1.sunk | while | flops 2 | bytes 4201 | solution.py:29
  334.7 23.1 %while.3 = (s32[]{:T(128)}, bf16[8,32]{1,0:T(8,128)(2,1)S(1)}, s32[16,2]{0,1:T(2,128)S(1)}, bf16[16,8,16]{2,1,0:T(8,128)(2,1)S(1)}, s32[]{:T(128)}) while((s32[]{:T(128)}, bf16[8,32]{1,0:T(8,128)(2,1)S(1)}, s32[16,2]{0,1:T(2,128)S(1)}, bf16[16,8,16]{2,1,0:T(8,128)(2,1)S(1)}, s32[]{:T(128)}) %tuple.92), condition=%wide.while_cond, body=%wide.while_body.sunk | while | flops 2 | bytes 4201 | solution.py:29
  357.9 70.0 %all-gather.3.cloned.1.call-done = bf16[8,3,2,16,1024]{4,3,0,2,1:T(8,128)(2,1)} async-done(((bf16[8,3,2,16,128]{4,3,0,2,1:T(8,128)(2,1)}), bf16[8,3,2,16,1024]{4,3,0,2,1:T(8,128)(2,1)}) %all-gather.3.cloned.1.call-update) | async-done | bytes 1572880 | tf_op jit(solution)/shard_map/all_gather | solution.py:117
  427.8 4.2 fusion.6
  432.3 7.6 %collective-permute-start.3 = (bf16[1,4,34,1]{3,1,2,0:T(4,128)(2,1)S(1)}, bf16[1,4,34,1]{3,1,2,0:T(4,128)(2,1)S(1)}, u32[]{:S(2)}, u32[]{:S(2)}) collective-permute-start(bf16[1,4,34,1]{3,1,2,0:T(4,128)(2,1)S(1)} %get-tuple-element.124), channel_id=1, source_target_pairs={{8,0},{16,8},{24,16},{32,24},{40,32},{48,40},{56,48},{9,1},{17,9},... | collective-permute-start | bytes 824 | tf_op jit(solution)/shard_map/ppermute | solution.py:19
  441.9 16.2 %collective-permute-done.2 = bf16[1,4,34,1]{3,1,2,0:T(4,128)(2,1)S(1)} collective-permute-done((bf16[1,4,34,1]{3,1,2,0:T(4,128)(2,1)S(1)}, bf16[1,4,34,1]{3,1,2,0:T(4,128)(2,1)S(1)}, u32[]{:S(2)}, u32[]{:S(2)}) %collective-permute-start.2) | collective-permute-done | bytes 304 | tf_op jit(solution)/shard_map/ppermute | solution.py:18
  460.7 3.9 collective-permute-start.8
  470.7 6.9 %collective-permute-done.9 = f32[3,4,34,1]{3,1,2,0:T(4,128)S(1)} collective-permute-done((f32[3,4,34,1]{3,1,2,0:T(4,128)S(1)}, f32[3,4,34,1]{3,1,2,0:T(4,128)S(1)}, u32[]{:S(2)}, u32[]{:S(2)}) %collective-permute-start.9) | collective-permute-done | bytes 1664 | tf_op jit(solution)/shard_map/ppermute | solution.py:19
  477.6 14.5 %collective-permute-done.8 = f32[3,4,34,1]{3,1,2,0:T(4,128)S(1)} collective-permute-done((f32[3,4,34,1]{3,1,2,0:T(4,128)S(1)}, f32[3,4,34,1]{3,1,2,0:T(4,128)S(1)}, u32[]{:S(2)}, u32[]{:S(2)}) %collective-permute-start.8) | collective-permute-done | bytes 1664 | tf_op jit(solution)/shard_map/ppermute | solution.py:18
  493.5 14.6 %collective-permute-start.11 = (f32[3,1,34,258]{3,2,1,0:T(8,128)}, f32[3,1,34,258]{3,2,1,0:T(8,128)}, u32[]{:S(2)}, u32[]{:S(2)}) collective-permute-start(f32[3,1,34,258]{3,2,1,0:T(8,128)} %get-tuple-element.96), channel_id=1, source_target_pairs={{1,0},{2,1},{3,2},{4,3},{5,4},{6,5},{7,6},{9,8},{10,9},{11,10},{12... | collective-permute-start | bytes 315800 | tf_op jit(solution)/shard_map/ppermute | solution.py:19
  523.8 3.6 collective-permute-start.13
  530.9 4.1 collective-permute-start.14
  538.3 13.0 %collective-permute-done.14 = f32[3,4,34,1]{3,1,2,0:T(4,128)S(1)} collective-permute-done((f32[3,4,34,1]{3,1,2,0:T(4,128)S(1)}, f32[3,4,34,1]{3,1,2,0:T(4,128)S(1)}, u32[]{:S(2)}, u32[]{:S(2)}) %collective-permute-start.14) | collective-permute-done | bytes 1664 | tf_op jit(solution)/shard_map/ppermute | solution.py:18
  552.0 14.2 %collective-permute-start.17 = (f32[3,1,34,258]{3,2,1,0:T(8,128)S(1)}, f32[3,1,34,258]{3,2,1,0:T(8,128)S(1)}, u32[]{:S(2)}, u32[]{:S(2)}) collective-permute-start(f32[3,1,34,258]{3,2,1,0:T(8,128)S(1)} %get-tuple-element.94), channel_id=1, source_target_pairs={{1,0},{2,1},{3,2},{4,3},{5,4},{6,5},{7,6},{9,8},{10,9},{11,10},{12... | collective-permute-start | bytes 315800 | tf_op jit(solution)/shard_map/ppermute | solution.py:19
  570.3 4.1 collective-permute-done.16
  584.6 3.9 collective-permute-start.20
  589.2 4.0 collective-permute-done.21
  593.2 15.2 %collective-permute-done.20 = f32[3,4,34,1]{3,1,2,0:T(4,128)S(1)} collective-permute-done((f32[3,4,34,1]{3,1,2,0:T(4,128)S(1)}, f32[3,4,34,1]{3,1,2,0:T(4,128)S(1)}, u32[]{:S(2)}, u32[]{:S(2)}) %collective-permute-start.20) | collective-permute-done | bytes 1664 | tf_op jit(solution)/shard_map/ppermute | solution.py:18
  609.1 12.2 %collective-permute-start.23 = (f32[3,1,34,258]{3,2,1,0:T(8,128)S(1)}, f32[3,1,34,258]{3,2,1,0:T(8,128)S(1)}, u32[]{:S(2)}, u32[]{:S(2)}) collective-permute-start(f32[3,1,34,258]{3,2,1,0:T(8,128)S(1)} %get-tuple-element.92), channel_id=1, source_target_pairs={{1,0},{2,1},{3,2},{4,3},{5,4},{6,5},{7,6},{9,8},{10,9},{11,10},{12... | collective-permute-start | bytes 315800 | tf_op jit(solution)/shard_map/ppermute | solution.py:19
  625.4 4.1 collective-permute-done.22
  (640 shorter events, 365.7 us)
Async XLA Ops:
  46.3 287.5 %all-to-all-start = ((bf16[8,3,2,16,128]{4,3,2,1,0:T(8,128)(2,1)}), bf16[8,3,2,16,128]{4,3,2,1,0:T(8,128)(2,1)S(1)}, u32[]{:S(2)}, u32[]{:S(2)}) async-start(bf16[8,3,2,16,128]{4,3,2,1,0:T(8,128)(2,1)} %stack.14), calls=%async_computation | async-start | bytes 393216 | tf_op jit(solution)/shard_map/all_to_all | solution.py:108
  51.1 376.7 %all-gather.3.cloned.1.call-start = ((), (), s32[]{:S(2)}) async-start(), calls=%async_computation.1 | async-start | bytes 1769472 | tf_op jit(solution)/shard_map/all_gather | solution.py:117
  51.1 407.4 %collective-permute-start.7 = (f32[3,4,1,256]{3,1,2,0:T(4,128)S(1)}, f32[3,4,1,256]{3,1,2,0:T(4,128)S(1)}, u32[]{:S(2)}, u32[]{:S(2)}) collective-permute-start(f32[3,4,1,256]{3,1,2,0:T(4,128)S(1)} %copy.557), channel_id=1, source_target_pairs={{64,0},{128,64},{192,128},{256,192},{320,256},{384,320},{448,384},... | collective-permute-start | bytes 36872 | tf_op jit(solution)/shard_map/ppermute | solution.py:19
  53.2 405.1 %collective-permute-start.6 = (f32[3,4,1,256]{3,1,2,0:T(4,128)S(1)}, f32[3,4,1,256]{3,1,2,0:T(4,128)S(1)}, u32[]{:S(2)}, u32[]{:S(2)}) collective-permute-start(f32[3,4,1,256]{3,1,2,0:T(4,128)S(1)} %copy.558), channel_id=1, source_target_pairs={{0,64},{64,128},{128,192},{192,256},{256,320},{320,384},{384,448},... | collective-permute-start | bytes 36872 | tf_op jit(solution)/shard_map/ppermute | solution.py:18
  55.5 376.6 %collective-permute-start = (bf16[1,4,1,256]{3,2,1,0:T(2,128)(2,1)S(1)}, bf16[1,4,1,256]{3,2,1,0:T(2,128)(2,1)S(1)}, u32[]{:S(2)}, u32[]{:S(2)}) collective-permute-start(bf16[1,4,1,256]{3,2,1,0:T(2,128)(2,1)S(1)} %get-tuple-element.126), channel_id=1, source_target_pairs={{0,64},{64,128},{128,192},{192,256},{256,320},{320,384},{384,448},... | collective-permute-start | bytes 6152 | tf_op jit(solution)/shard_map/ppermute | solution.py:18
  58.8 373.4 %collective-permute-start.1 = (bf16[1,4,1,256]{3,2,1,0:T(2,128)(2,1)S(1)}, bf16[1,4,1,256]{3,2,1,0:T(2,128)(2,1)S(1)}, u32[]{:S(2)}, u32[]{:S(2)}) collective-permute-start(bf16[1,4,1,256]{3,2,1,0:T(2,128)(2,1)S(1)} %get-tuple-element.125), channel_id=1, source_target_pairs={{64,0},{128,64},{192,128},{256,192},{320,256},{384,320},{448,384},... | collective-permute-start | bytes 6152 | tf_op jit(solution)/shard_map/ppermute | solution.py:19
  334.7 177.8 %all-gather.5.cloned.1.call-start = ((), (), s32[]{:S(2)}) async-start(), calls=%async_computation.2 | async-start | bytes 1769472 | tf_op jit(solution)/shard_map/all_gather | solution.py:128
  432.3 9.6 %collective-permute-start.3 = (bf16[1,4,34,1]{3,1,2,0:T(4,128)(2,1)S(1)}, bf16[1,4,34,1]{3,1,2,0:T(4,128)(2,1)S(1)}, u32[]{:S(2)}, u32[]{:S(2)}) collective-permute-start(bf16[1,4,34,1]{3,1,2,0:T(4,128)(2,1)S(1)} %get-tuple-element.124), channel_id=1, source_target_pairs={{8,0},{16,8},{24,16},{32,24},{40,32},{48,40},{56,48},{9,1},{17,9},... | collective-permute-start | bytes 824 | tf_op jit(solution)/shard_map/ppermute | solution.py:19
  439.9 18.2 %collective-permute-start.2 = (bf16[1,4,34,1]{3,1,2,0:T(4,128)(2,1)S(1)}, bf16[1,4,34,1]{3,1,2,0:T(4,128)(2,1)S(1)}, u32[]{:S(2)}, u32[]{:S(2)}) collective-permute-start(bf16[1,4,34,1]{3,1,2,0:T(4,128)(2,1)S(1)} %get-tuple-element.123), channel_id=1, source_target_pairs={{0,8},{8,16},{16,24},{24,32},{32,40},{40,48},{48,56},{1,9},{9,17},... | collective-permute-start | bytes 824 | tf_op jit(solution)/shard_map/ppermute | solution.py:18
  458.8 18.8 %collective-permute-start.9 = (f32[3,4,34,1]{3,1,2,0:T(4,128)S(1)}, f32[3,4,34,1]{3,1,2,0:T(4,128)S(1)}, u32[]{:S(2)}, u32[]{:S(2)}) collective-permute-start(f32[3,4,34,1]{3,1,2,0:T(4,128)S(1)} %get-tuple-element.108), channel_id=1, source_target_pairs={{8,0},{16,8},{24,16},{32,24},{40,32},{48,40},{56,48},{9,1},{17,9},... | collective-permute-start | bytes 4904 | tf_op jit(solution)/shard_map/ppermute | solution.py:19
  460.7 31.4 %collective-permute-start.8 = (f32[3,4,34,1]{3,1,2,0:T(4,128)S(1)}, f32[3,4,34,1]{3,1,2,0:T(4,128)S(1)}, u32[]{:S(2)}, u32[]{:S(2)}) collective-permute-start(f32[3,4,34,1]{3,1,2,0:T(4,128)S(1)} %get-tuple-element.107), channel_id=1, source_target_pairs={{0,8},{8,16},{16,24},{24,32},{32,40},{40,48},{48,56},{1,9},{9,17},... | collective-permute-start | bytes 4904 | tf_op jit(solution)/shard_map/ppermute | solution.py:18
  464.7 46.6 %collective-permute-start.5 = (bf16[1,1,34,258]{3,2,1,0:T(8,128)(2,1)S(1)}, bf16[1,1,34,258]{3,2,1,0:T(8,128)(2,1)S(1)}, u32[]{:S(2)}, u32[]{:S(2)}) collective-permute-start(bf16[1,1,34,258]{3,2,1,0:T(8,128)(2,1)S(1)} %copy.559), channel_id=1, source_target_pairs={{1,0},{2,1},{3,2},{4,3},{5,4},{6,5},{7,6},{9,8},{10,9},{11,10},{12... | collective-permute-start | bytes 52640 | tf_op jit(solution)/shard_map/ppermute | solution.py:19
  467.6 43.8 %collective-permute-start.4 = (bf16[1,1,34,258]{3,2,1,0:T(8,128)(2,1)S(1)}, bf16[1,1,34,258]{3,2,1,0:T(8,128)(2,1)S(1)}, u32[]{:S(2)}, u32[]{:S(2)}) collective-permute-start(bf16[1,1,34,258]{3,2,1,0:T(8,128)(2,1)S(1)} %copy.560), channel_id=1, source_target_pairs={{0,1},{1,2},{2,3},{3,4},{4,5},{5,6},{6,7},{8,9},{9,10},{10,11},{11... | collective-permute-start | bytes 52640 | tf_op jit(solution)/shard_map/ppermute | solution.py:18
  493.5 25.9 %collective-permute-start.11 = (f32[3,1,34,258]{3,2,1,0:T(8,128)}, f32[3,1,34,258]{3,2,1,0:T(8,128)}, u32[]{:S(2)}, u32[]{:S(2)}) collective-permute-start(f32[3,1,34,258]{3,2,1,0:T(8,128)} %get-tuple-element.96), channel_id=1, source_target_pairs={{1,0},{2,1},{3,2},{4,3},{5,4},{6,5},{7,6},{9,8},{10,9},{11,10},{12... | collective-permute-start | bytes 315800 | tf_op jit(solution)/shard_map/ppermute | solution.py:19
  508.0 11.4 %collective-permute-start.10 = (f32[3,1,34,258]{3,2,1,0:T(8,128)}, f32[3,1,34,258]{3,2,1,0:T(8,128)}, u32[]{:S(2)}, u32[]{:S(2)}) collective-permute-start(f32[3,1,34,258]{3,2,1,0:T(8,128)} %get-tuple-element.95), channel_id=1, source_target_pairs={{0,1},{1,2},{2,3},{3,4},{4,5},{5,6},{6,7},{8,9},{9,10},{10,11},{11... | collective-permute-start | bytes 315800 | tf_op jit(solution)/shard_map/ppermute | solution.py:18
  529.0 9.3 %collective-permute-start.15 = (f32[3,4,34,1]{3,1,2,0:T(4,128)S(1)}, f32[3,4,34,1]{3,1,2,0:T(4,128)S(1)}, u32[]{:S(2)}, u32[]{:S(2)}) collective-permute-start(f32[3,4,34,1]{3,1,2,0:T(4,128)S(1)} %get-tuple-element.104), channel_id=1, source_target_pairs={{8,0},{16,8},{24,16},{32,24},{40,32},{48,40},{56,48},{9,1},{17,9},... | collective-permute-start | bytes 4904 | tf_op jit(solution)/shard_map/ppermute | solution.py:19
  530.9 20.4 %collective-permute-start.14 = (f32[3,4,34,1]{3,1,2,0:T(4,128)S(1)}, f32[3,4,34,1]{3,1,2,0:T(4,128)S(1)}, u32[]{:S(2)}, u32[]{:S(2)}) collective-permute-start(f32[3,4,34,1]{3,1,2,0:T(4,128)S(1)} %get-tuple-element.103), channel_id=1, source_target_pairs={{0,8},{8,16},{16,24},{24,32},{32,40},{40,48},{48,56},{1,9},{9,17},... | collective-permute-start | bytes 4904 | tf_op jit(solution)/shard_map/ppermute | solution.py:18
  552.0 18.3 %collective-permute-start.17 = (f32[3,1,34,258]{3,2,1,0:T(8,128)S(1)}, f32[3,1,34,258]{3,2,1,0:T(8,128)S(1)}, u32[]{:S(2)}, u32[]{:S(2)}) collective-permute-start(f32[3,1,34,258]{3,2,1,0:T(8,128)S(1)} %get-tuple-element.94), channel_id=1, source_target_pairs={{1,0},{2,1},{3,2},{4,3},{5,4},{6,5},{7,6},{9,8},{10,9},{11,10},{12... | collective-permute-start | bytes 315800 | tf_op jit(solution)/shard_map/ppermute | solution.py:19
  566.2 8.2 %collective-permute-start.16 = (f32[3,1,34,258]{3,2,1,0:T(8,128)S(1)}, f32[3,1,34,258]{3,2,1,0:T(8,128)S(1)}, u32[]{:S(2)}, u32[]{:S(2)}) collective-permute-start(f32[3,1,34,258]{3,2,1,0:T(8,128)S(1)} %get-tuple-element.93), channel_id=1, source_target_pairs={{0,1},{1,2},{2,3},{3,4},{4,5},{5,6},{6,7},{8,9},{9,10},{10,11},{11... | collective-permute-start | bytes 315800 | tf_op jit(solution)/shard_map/ppermute | solution.py:18
  575.5 5.6 collective-permute-start.18
  582.7 10.6 %collective-permute-start.21 = (f32[3,4,34,1]{3,1,2,0:T(4,128)S(1)}, f32[3,4,34,1]{3,1,2,0:T(4,128)S(1)}, u32[]{:S(2)}, u32[]{:S(2)}) collective-permute-start(f32[3,4,34,1]{3,1,2,0:T(4,128)S(1)} %get-tuple-element.100), channel_id=1, source_target_pairs={{8,0},{16,8},{24,16},{32,24},{40,32},{48,40},{56,48},{9,1},{17,9},... | collective-permute-start | bytes 4904 | tf_op jit(solution)/shard_map/ppermute | solution.py:19
  584.6 23.9 %collective-permute-start.20 = (f32[3,4,34,1]{3,1,2,0:T(4,128)S(1)}, f32[3,4,34,1]{3,1,2,0:T(4,128)S(1)}, u32[]{:S(2)}, u32[]{:S(2)}) collective-permute-start(f32[3,4,34,1]{3,1,2,0:T(4,128)S(1)} %get-tuple-element.99), channel_id=1, source_target_pairs={{0,8},{8,16},{16,24},{24,32},{32,40},{40,48},{48,56},{1,9},{9,17},... | collective-permute-start | bytes 4904 | tf_op jit(solution)/shard_map/ppermute | solution.py:18
  609.1 16.3 %collective-permute-start.23 = (f32[3,1,34,258]{3,2,1,0:T(8,128)S(1)}, f32[3,1,34,258]{3,2,1,0:T(8,128)S(1)}, u32[]{:S(2)}, u32[]{:S(2)}) collective-permute-start(f32[3,1,34,258]{3,2,1,0:T(8,128)S(1)} %get-tuple-element.92), channel_id=1, source_target_pairs={{1,0},{2,1},{3,2},{4,3},{5,4},{6,5},{7,6},{9,8},{10,9},{11,10},{12... | collective-permute-start | bytes 315800 | tf_op jit(solution)/shard_map/ppermute | solution.py:19
  621.3 8.3 %collective-permute-start.22 = (f32[3,1,34,258]{3,2,1,0:T(8,128)S(1)}, f32[3,1,34,258]{3,2,1,0:T(8,128)S(1)}, u32[]{:S(2)}, u32[]{:S(2)}) collective-permute-start(f32[3,1,34,258]{3,2,1,0:T(8,128)S(1)} %get-tuple-element.91), channel_id=1, source_target_pairs={{0,1},{1,2},{2,3},{3,4},{4,5},{5,6},{6,7},{8,9},{9,10},{10,11},{11... | collective-permute-start | bytes 315800 | tf_op jit(solution)/shard_map/ppermute | solution.py:18
  (14 other events, 747.3 us)
Sparse Core Ops, SparseCore 0:
  334.8 92.9 all-gather.2
  432.2 70.8 all-gather.4
